TPU v7x, 32 devices: a whole 2x2x4 slice. The times are simulated.
32 devices in a mesh: groups: 2 (over y), tiles: 16 (over z, x, core).
Axes of the slice: x: 2, y: 2, z: 4, core: 2. Of those that a mesh axis runs over, the one named last changes fastest.
Arguments:
- raw: bfloat16 [16, 256, 2048], P(None, ('groups', 'tiles')), parts along dimension 1, may hold values from -40 to 40, as said below
- fir: float32 [64], replicated, may hold values from -0.75 to 0.75
- keep: int32 [16, 256], P(None, ('groups', 'tiles')), parts along dimension 1, may hold values 0 or 1
- table: int32 [16, 2], replicated, may hold values from 0 to 0, as said below
Outputs:
- stacks: bfloat16 [32, 128, 128, 256], P(('groups', 'tiles')), parts along dimension 0
There are 2 independent parts, one for each index of `groups`. A program takes and returns all parts, laid end to end along the dimension named above; an argument that names none is the same for every part. Nothing has to cross between parts.
Inputs may be any that keep to these rules, and one draw needn't show every extreme that they name: `table`: each row holds r <= c. `raw`: a common motion of all channels plus independent noise.
All inputs are finite; a program needn't handle non-finite values. No bound on the sum of `keep` on one device may be relied on, other than what follows from the above.
Results may differ from a plain program's by a relative error of at most 0.0053.
Values may be sent and summed in bfloat16 or wider, within the bound.
A program may use at most 128 MiB of HBM per device.

v0:
```python
import jax
import jax.numpy as jnp
from jax import lax
from jax.sharding import PartitionSpec as P

WINDOWS = 16
TILE = 128
SEG = 512
LAGS = 256
TAPS = 64
DEC = 4
RAW = 2048
NBIN = 256


def filter_band(fir):
    period = 2 * RAW + TAPS
    pattern = jnp.concatenate([fir[:1], jnp.zeros((period - TAPS,), jnp.float32), fir[1:][::-1]])
    tiled = jnp.tile(pattern, SEG)[: SEG * (period - DEC)].reshape(SEG, period - DEC)
    return tiled[:, :RAW]


def filter_block(raw, fir):
    band = filter_band(fir)
    return jnp.einsum("wcm,nm->wcn", raw.astype(jnp.float32), band, precision=lax.Precision.HIGHEST)


def dft_tables():
    steps = jnp.arange(SEG, dtype=jnp.int32)
    freqs = jnp.arange(NBIN, dtype=jnp.int32)
    angle = 2.0 * jnp.pi / SEG * jnp.mod(steps[:, None] * freqs[None, :], SEG).astype(jnp.float32)
    return (jnp.cos(angle), jnp.sin(angle))


def whiten(decimated, keep):
    cosine, sine = dft_tables()
    real_part = jnp.einsum("wcn,nf->wcf", decimated, cosine, precision=lax.Precision.HIGHEST)
    imag_part = -jnp.einsum("wcn,nf->wcf", decimated, sine, precision=lax.Precision.HIGHEST)
    power = real_part * real_part + imag_part * imag_part
    level = jnp.mean(power, -1, keepdims=True)
    scale = keep.astype(jnp.float32)[..., None] / jnp.sqrt(0.5 * power + 0.5 * level + 1e-05)
    return jnp.concatenate([real_part * scale, imag_part * scale], -1).astype(jnp.bfloat16)


def cross_tile(rows, cols):
    half = rows.shape[-1] // 2
    row_re, row_im = (rows[..., :half], rows[..., half:])
    col_re, col_im = (cols[..., :half], cols[..., half:])
    cross_re = jnp.einsum("wif,wjf->ijf", row_re, col_re, preferred_element_type=jnp.float32)
    cross_re = cross_re + jnp.einsum(
        "wif,wjf->ijf", row_im, col_im, preferred_element_type=jnp.float32
    )
    cross_im = jnp.einsum("wif,wjf->ijf", row_re, col_im, preferred_element_type=jnp.float32)
    cross_im = cross_im - jnp.einsum(
        "wif,wjf->ijf", row_im, col_re, preferred_element_type=jnp.float32
    )
    return jnp.concatenate([cross_re, cross_im], -1).astype(jnp.bfloat16)


def lag_rows(freqs, imaginary):
    shifts = jnp.arange(LAGS, dtype=jnp.int32) - LAGS // 2
    angle = 2.0 * jnp.pi / SEG * jnp.mod(freqs[:, None] * shifts[None, :], SEG).astype(jnp.float32)
    weight = jnp.where(freqs == 0, 1.0, 2.0).astype(jnp.float32)[:, None] / jnp.sqrt(
        jnp.float32(WINDOWS * NBIN)
    )
    return jnp.where(imaginary[:, None], -weight * jnp.sin(angle), weight * jnp.cos(angle)).astype(
        jnp.bfloat16
    )


def local(raw, fir, keep, table):
    devices = lax.axis_size("tiles")
    filtered = filter_block(raw, fir)
    channel_sum = lax.psum(jnp.sum(filtered, 1), "tiles")
    common = channel_sum[:, None, :] / (raw.shape[1] * devices)
    whitened = whiten(filtered - common, keep)
    entry = table[lax.axis_index("tiles")]
    row_base = entry[0] * TILE
    col_base = entry[1] * TILE
    offsets = jnp.arange(TILE, dtype=jnp.int32)
    piece = lax.all_gather(whitened, "tiles", axis=1, tiled=True)
    places = jnp.arange(piece.shape[1], dtype=jnp.int32)
    pick_rows = (places[None, :] == row_base + offsets[:, None]).astype(jnp.bfloat16)
    pick_cols = (places[None, :] == col_base + offsets[:, None]).astype(jnp.bfloat16)
    add_rows = jnp.einsum("in,wnf->wif", pick_rows, piece, preferred_element_type=jnp.float32)
    add_cols = jnp.einsum("in,wnf->wif", pick_cols, piece, preferred_element_type=jnp.float32)
    rows = add_rows.astype(jnp.bfloat16)
    cols = add_cols.astype(jnp.bfloat16)
    cross = cross_tile(rows, cols).reshape(TILE * TILE, 2 * NBIN)
    freqs = jnp.concatenate([jnp.arange(NBIN, dtype=jnp.int32)] * 2)
    imaginary = jnp.arange(2 * NBIN, dtype=jnp.int32) >= NBIN
    lags = lag_rows(freqs, imaginary)
    stacked = jnp.dot(cross, lags, preferred_element_type=jnp.float32).astype(jnp.bfloat16)
    return stacked.reshape(1, TILE, TILE, LAGS)


def solution(mesh):
    placed = (P(None, ("groups", "tiles"), None), P(), P(None, ("groups", "tiles")), P())
    return jax.shard_map(
        local,
        mesh=mesh,
        in_specs=placed,
        out_specs=P(("groups", "tiles"), None, None, None),
        check_vma=False,
    )
```

profile of v0, /device:TPU:0, one launch (start us, length us, event | category | flops | bytes accessed | tf_op | source)
XLA Modules:
  0.0 251.8 jit_solution(16928799047254272326)
XLA Ops:
  6.5 0.8 slice.33
  7.4 0.7 concatenate.26
  8.2 3.9 %tile.4 = f32[512,4160]{1,0:T(8,128)} broadcast(f32[4160]{0:T(1024)S(1)} %concatenate.26), dimensions={1} | broadcast | bytes 8536320 | tf_op jit(solution)/shard_map/tile | solution.py:19
  12.0 10.0 %tile.10 = f32[2129920]{0:T(1024)} reshape(f32[512,4160]{1,0:T(8,128)} %tile.4) | data formatting | bytes 17039360 | tf_op jit(solution)/shard_map/tile | solution.py:19
  22.0 7.8 %slice.42 = f32[2127872]{0:T(1024)} slice(f32[2129920]{0:T(1024)} %tile.10), slice={[0:2127872]} | slice | bytes 17022976 | tf_op jit(solution)/shard_map/slice | solution.py:19
  29.8 14.4 %reshape.66 = f32[512,4156]{1,0:T(8,128)} reshape(f32[2127872]{0:T(1024)} %slice.42) | data formatting | bytes 17022976 | tf_op jit(solution)/shard_map/reshape | solution.py:19
  44.2 4.8 %fusion.70 = (f32[16,512]{1,0:T(8,128)S(1)}, f32[16,8,512]{2,0,1:T(8,128)S(1)}) fusion(bf16[16,8,2048]{2,1,0:T(8,128)(2,1)S(1)} %copy-done, f32[512,4156]{1,0:T(8,128)} %reshape.66), kind=kOutput, calls=%fused_computation.98 | convolution fusion | flops 1610670080 | bytes 5013504 | tf_op jit(solution)/shard_map/wcm,nm->wcn/dot_general | solution.py:25
  49.0 62.9 %psum.7 = f32[16,512]{1,0:T(8,128)S(1)} all-reduce(f32[16,512]{1,0:T(8,128)S(1)} %get-tuple-element.15), channel_id=1, replica_groups=mesh['groups'=2,'tiles'=16] {'tiles'}, use_global_device_ids=true, to_apply=%region_1.0 | all-reduce | flops 8192 | bytes 65536 | tf_op jit(solution)/shard_map/psum | solution.py:74
  112.0 2.4 fusion.25
  114.4 2.5 fusion.46
  117.0 0.1 multiply_convert_fusion.1
  117.1 0.7 pad_maximum_fusion
  117.9 0.6 fusion.69
  119.8 36.6 %all-gather.2.cloned.1.call-done = bf16[16,128,512]{2,1,0:T(8,128)(2,1)} async-done(((bf16[16,8,512]{2,1,0:T(8,128)(2,1)}), bf16[16,128,512]{2,1,0:T(8,128)(2,1)}) %all-gather.2.cloned.1.call-update) | async-done | bytes 2097168 | tf_op jit(solution)/shard_map/all_gather | solution.py:81
  156.4 2.4 convert_bitcast_fusion
  158.8 2.4 convert_bitcast_fusion.1
  161.2 0.3 fusion.67
  161.5 8.1 %fusion.13 = f32[256,128,128]{2,1,0:T(8,128)} fusion(bf16[16,128,256]{1,2,0:T(8,128)(2,1)S(1)} %get-tuple-element.19, bf16[16,128,256]{1,2,0:T(8,128)(2,1)S(1)} %get-tuple-element.5), kind=kOutput, calls=%fused_computation.22 | convolution fusion | flops 134217728 | bytes 18874368 | tf_op jit(solution)/shard_map/wif,wjf->ijf/dot_general | solution.py:49
  169.6 8.1 %fusion.9 = f32[256,128,128]{2,1,0:T(8,128)} fusion(bf16[16,128,256]{1,2,0:T(8,128)(2,1)S(1)} %get-tuple-element.6, bf16[16,128,256]{1,2,0:T(8,128)(2,1)S(1)} %get-tuple-element.19), kind=kOutput, calls=%fused_computation.18 | convolution fusion | flops 134217728 | bytes 18874368 | tf_op jit(solution)/shard_map/wif,wjf->ijf/dot_general | solution.py:53
  177.6 12.9 %fusion.3 = bf16[128,128,256]{0,1,2:T(8,128)(2,1)} fusion(f32[256,128,128]{2,1,0:T(8,128)} %fusion.13, bf16[16,128,256]{1,2,0:T(8,128)(2,1)S(1)} %get-tuple-element.20, bf16[16,128,256]{1,2,0:T(8,128)(2,1)S(1)} %get-tuple-element.6), kind=kOutput, calls=%fused_computation.6 | convolution fusion | flops 142606336 | bytes 27262976 | tf_op jit(solution)/shard_map/wif,wjf->ijf/dot_general | solution.py:50
  190.5 13.5 %copy.25 = bf16[128,128,256]{2,1,0:T(8,128)(2,1)} copy(bf16[128,128,256]{0,1,2:T(8,128)(2,1)} %fusion.3) | data formatting | bytes 16777216 | tf_op jit(solution)/shard_map/add | solution.py:50
  204.0 12.9 %fusion.4 = bf16[128,128,256]{0,1,2:T(8,128)(2,1)} fusion(f32[256,128,128]{2,1,0:T(8,128)} %fusion.9, bf16[16,128,256]{1,2,0:T(8,128)(2,1)S(1)} %get-tuple-element.20, bf16[16,128,256]{1,2,0:T(8,128)(2,1)S(1)} %get-tuple-element.5), kind=kOutput, calls=%fused_computation.7 | convolution fusion | flops 142606336 | bytes 27262976 | tf_op jit(solution)/shard_map/wif,wjf->ijf/dot_general | solution.py:54
  216.9 13.5 %copy.30 = bf16[128,128,256]{2,1,0:T(8,128)(2,1)} copy(bf16[128,128,256]{0,1,2:T(8,128)(2,1)} %fusion.4) | data formatting | bytes 16777216 | tf_op jit(solution)/shard_map/sub | solution.py:54
  230.4 14.5 %convolution_convert_fusion = bf16[16384,256]{1,0:T(8,128)(2,1)} fusion(bf16[16384,256]{1,0:T(8,128)(2,1)} %bitcast.40, bf16[16384,256]{1,0:T(8,128)(2,1)} %bitcast.39, f32[512]{0:T(512)S(1)} %get-tuple-element.12, s32[256]{0:T(256)S(1)} %iota_add_fusion, s32[512]{0:T(512)S(1)} %pad_add_fusion, f32[512]{0:T(512)S(1)} %get-tuple-element.11, ...), kind=kOutput, calls=%fused_computation | convolution fusion | flops 4335075328 | bytes 25173504 | tf_op jit(solution)/shard_map/dot_general | solution.py:93
  (25 shorter events, 0.4 us)
Async XLA Ops:
  6.5 37.6 %copy-start = (bf16[16,8,2048]{2,1,0:T(8,128)(2,1)S(1)}, bf16[16,8,2048]{2,1,0:T(8,128)(2,1)}, u32[]{:S(2)}) copy-start(bf16[16,8,2048]{2,1,0:T(8,128)(2,1)} %param.4) | copy-start | bytes 1572868
  6.5 149.9 %all-gather.2.cloned.1.call-start = ((), (), s32[]{:S(2)}) async-start(), calls=%async_computation | async-start | bytes 2228224 | tf_op jit(solution)/shard_map/all_gather | solution.py:81
  44.2 72.7 %copy-start.2 = (s32[16,8]{0,1:T(8,128)S(1)}, s32[16,8]{0,1:T(8,128)}, u32[]{:S(2)}) copy-start(s32[16,8]{0,1:T(8,128)} %param.6) | copy-start | bytes 1540
  44.2 73.6 %copy-start.3 = (s32[16,2]{0,1:T(2,128)S(1)}, s32[16,2]{0,1:T(2,128)}, u32[]{:S(2)}) copy-start(s32[16,2]{0,1:T(2,128)} %param.7) | copy-start | bytes 388
  230.4 14.5 %copy-start.1 = (bf16[16,8,2048]{2,1,0:T(8,128)(2,1)S(1)}, bf16[16,8,2048]{2,1,0:T(8,128)(2,1)}, u32[]{:S(2)}) copy-start(bf16[16,8,2048]{2,1,0:T(8,128)(2,1)} %param.4) | copy-start | bytes 1572868
Sparse Core Ops, SparseCore 0:
  117.9 38.4 all-gather.1
where the time goes:
time: 253 us; the launch traced here: 252 us
  matrix products  71 us (28%)
  local copies, waits for them, and re-layouts  65.6 us (26%)
  blocking collectives  62.9 us (25%)
  waiting for transfers between devices  36.6 us (14%)
  between operations  14.8 us (6%)
    psum x1, blocking collectives, local(): channel_sum = lax.psum(jnp.sum(filtered, 1), 'tiles')  62.9 us
    all_gather x1, waiting for transfers between devices, local(): piece = lax.all_gather(whitened, 'tiles', axis=1, tiled=True)  36.6 us
    dot_general x1, matrix products, local(): jnp.dot(cross, lags, preferred_element_type=jnp.float32)  14.5 us
    reshape x1, local copies, waits for them, and re-layouts, filter_band(): jnp.tile(pattern, SEG)[:SEG * (period - DEC)].reshape(SEG, period - DEC)  14.4 us
    another operation x2, local copies, waits for them, and re-layouts, filter_band(): jnp.tile(pattern, SEG)[:SEG * (period - DEC)].reshape(SEG, period - DEC)  13.8 us
    sub x1, local copies, waits for them, and re-layouts, cross_tile(): cross_im - jnp.einsum('wif,wjf->ijf', row_im, col_re, preferred_element_t...  13.5 us
    add x1, local copies, waits for them, and re-layouts, cross_tile(): cross_re + jnp.einsum('wif,wjf->ijf', row_im, col_im, preferred_element_t...  13.5 us
    dot_general x1, matrix products, cross_tile(): jnp.einsum('wif,wjf->ijf', row_im, col_re, preferred_element_type=jnp.flo...  12.9 us
  transfers between devices with their start and end apart: 1, of which 1 were waited for; matrix products, arithmetic and copies ran while one was open for 0% of the time, Pallas kernels for 0%

commit v1 on v0

--- a/solution.py
+++ b/solution.py
@@ -71,7 +71,7 @@
 def local(raw, fir, keep, table):
     devices = lax.axis_size("tiles")
     filtered = filter_block(raw, fir)
-    channel_sum = lax.psum(jnp.sum(filtered, 1), "tiles")
+    channel_sum = jnp.sum(lax.all_gather(jnp.sum(filtered, 1), "tiles"), axis=0)
     common = channel_sum[:, None, :] / (raw.shape[1] * devices)
     whitened = whiten(filtered - common, keep)
     entry = table[lax.axis_index("tiles")]

time: 253 us -> 215 us (0.85)
  blocking collectives: 62.9 us -> 24.8 us
    psum x1 -> x0, blocking collectives: 62.9 us -> none  [local(): channel_sum = lax.psum(jnp.sum(filtered, 1), 'tiles')]
    all_gather x0 -> x1, blocking collectives: none -> 24.8 us  [local(): channel_sum = jnp.sum(lax.all_gather(jnp.sum(filtered, 1), 'tiles'), axis=0)]
where the time goes in v1:
time: 215 us; the launch traced here: 214 us
  matrix products  71.2 us (33%)
  local copies, waits for them, and re-layouts  65.6 us (31%)
  waiting for transfers between devices  36.6 us (17%)
  blocking collectives  24.8 us (12%)
  between operations  14.9 us (7%)
    all_gather x1, waiting for transfers between devices, local(): piece = lax.all_gather(whitened, 'tiles', axis=1, tiled=True)  36.6 us
    all_gather x1, blocking collectives, local(): channel_sum = jnp.sum(lax.all_gather(jnp.sum(filtered, 1), 'tiles'), axis=0)  24.8 us
    dot_general x1, matrix products, local(): jnp.dot(cross, lags, preferred_element_type=jnp.float32)  14.5 us
    reshape x1, local copies, waits for them, and re-layouts, filter_band(): jnp.tile(pattern, SEG)[:SEG * (period - DEC)].reshape(SEG, period - DEC)  14.4 us
    another operation x2, local copies, waits for them, and re-layouts, filter_band(): jnp.tile(pattern, SEG)[:SEG * (period - DEC)].reshape(SEG, period - DEC)  13.8 us
    sub x1, local copies, waits for them, and re-layouts, cross_tile(): cross_im - jnp.einsum('wif,wjf->ijf', row_im, col_re, preferred_element_t...  13.5 us
    add x1, local copies, waits for them, and re-layouts, cross_tile(): cross_re + jnp.einsum('wif,wjf->ijf', row_im, col_im, preferred_element_t...  13.5 us
    dot_general x1, matrix products, cross_tile(): jnp.einsum('wif,wjf->ijf', row_im, col_re, preferred_element_type=jnp.flo...  12.9 us
  transfers between devices with their start and end apart: 1, of which 1 were waited for; matrix products, arithmetic and copies ran while one was open for 0% of the time, Pallas kernels for 0%

profile of v1, /device:TPU:0, one launch (start us, length us, event | category | flops | bytes accessed | tf_op | source)
XLA Modules:
  0.0 214.0 jit_solution(4773648077511945587)
XLA Ops:
  6.5 0.8 slice.33
  7.4 0.7 concatenate.26
  8.2 3.9 %tile.4 = f32[512,4160]{1,0:T(8,128)} broadcast(f32[4160]{0:T(1024)S(1)} %concatenate.26), dimensions={1} | broadcast | bytes 8536320 | tf_op jit(solution)/shard_map/tile | solution.py:19
  12.0 10.0 %tile.10 = f32[2129920]{0:T(1024)} reshape(f32[512,4160]{1,0:T(8,128)} %tile.4) | data formatting | bytes 17039360 | tf_op jit(solution)/shard_map/tile | solution.py:19
  22.0 7.8 %slice.42 = f32[2127872]{0:T(1024)} slice(f32[2129920]{0:T(1024)} %tile.10), slice={[0:2127872]} | slice | bytes 17022976 | tf_op jit(solution)/shard_map/slice | solution.py:19
  29.8 14.4 %reshape.68 = f32[512,4156]{1,0:T(8,128)} reshape(f32[2127872]{0:T(1024)} %slice.42) | data formatting | bytes 17022976 | tf_op jit(solution)/shard_map/reshape | solution.py:19
  44.2 4.8 %fusion.70 = (f32[16,512]{1,0:T(8,128)S(1)}, f32[16,8,512]{2,0,1:T(8,128)S(1)}) fusion(bf16[16,8,2048]{2,1,0:T(8,128)(2,1)S(1)} %copy-done, f32[512,4156]{1,0:T(8,128)} %reshape.68), kind=kOutput, calls=%fused_computation.98 | convolution fusion | flops 1610670080 | bytes 5013504 | tf_op jit(solution)/shard_map/wcm,nm->wcn/dot_general | solution.py:25
  49.0 24.8 %all-gather = f32[256,512]{1,0:T(8,128)S(1)} all-gather(f32[16,512]{1,0:T(8,128)S(1)} %get-tuple-element.15), channel_id=2, replica_groups=mesh['groups'=2,'tiles'=16] {'tiles'}, dimensions={0}, use_global_device_ids=true | all-gather | bytes 557056 | tf_op jit(solution)/shard_map/all_gather | solution.py:74
  73.9 2.4 %fusion.25 = f32[16,8,256]{2,1,0:T(8,128)S(1)} fusion(f32[16,8,512]{2,0,1:T(8,128)S(1)} %broadcast_subtract_fusion), kind=kOutput, calls=%fused_computation.39 | convolution fusion | flops 203161600 | bytes 393216 | tf_op jit(solution)/shard_map/wcn,nf->wcf/dot_general | solution.py:37
  76.3 2.5 %fusion.46 = (f32[16,8]{1,0:T(8,128)S(1)}, f32[16,8,256]{2,1,0:T(8,128)S(1)}) fusion(f32[16,8,256]{2,1,0:T(8,128)S(1)} %fusion.25, f32[16,8,512]{2,0,1:T(8,128)S(1)} %broadcast_subtract_fusion), kind=kOutput, calls=%fused_computation.65 | convolution fusion | flops 203292544 | bytes 524800 | tf_op jit(solution)/shard_map/wcn,nf->wcf/dot_general | solution.py:38
  78.9 0.1 multiply_convert_fusion.1
  79.0 0.7 pad_maximum_fusion
  79.7 0.6 fusion.69
  81.7 36.6 %all-gather.3.cloned.1.call-done = bf16[16,128,512]{2,1,0:T(8,128)(2,1)} async-done(((bf16[16,8,512]{2,1,0:T(8,128)(2,1)}), bf16[16,128,512]{2,1,0:T(8,128)(2,1)}) %all-gather.3.cloned.1.call-update) | async-done | bytes 2097168 | tf_op jit(solution)/shard_map/all_gather | solution.py:81
  118.3 2.4 %convert_bitcast_fusion = bf16[16,128,512]{1,2,0:T(8,128)(2,1)S(1)} fusion(bf16[16,128,512]{2,1,0:T(8,128)(2,1)} %all-gather.3.cloned.1.call-done, s32[128]{0:T(128)S(1)} %iota_add_fusion.1), kind=kOutput, calls=%fused_computation.10 | convolution fusion | flops 269500416 | bytes 4194816 | tf_op jit(solution)/shard_map/in,wnf->wif/dot_general | solution.py:85
  120.7 2.4 %convert_bitcast_fusion.1 = bf16[16,128,512]{1,2,0:T(8,128)(2,1)S(1)} fusion(bf16[16,128,512]{2,1,0:T(8,128)(2,1)} %all-gather.3.cloned.1.call-done, s32[128]{0:T(128)S(1)} %iota_add_fusion.2), kind=kOutput, calls=%fused_computation.11 | convolution fusion | flops 269500416 | bytes 4194816 | tf_op jit(solution)/shard_map/in,wnf->wif/dot_general | solution.py:86
  123.1 0.3 fusion.67
  123.4 8.3 %fusion.13 = f32[256,128,128]{2,1,0:T(8,128)} fusion(bf16[16,128,256]{1,2,0:T(8,128)(2,1)S(1)} %get-tuple-element.19, bf16[16,128,256]{1,2,0:T(8,128)(2,1)S(1)} %get-tuple-element.5), kind=kOutput, calls=%fused_computation.22 | convolution fusion | flops 134217728 | bytes 18874368 | tf_op jit(solution)/shard_map/wif,wjf->ijf/dot_general | solution.py:49
  131.7 8.1 %fusion.9 = f32[256,128,128]{2,1,0:T(8,128)} fusion(bf16[16,128,256]{1,2,0:T(8,128)(2,1)S(1)} %get-tuple-element.6, bf16[16,128,256]{1,2,0:T(8,128)(2,1)S(1)} %get-tuple-element.19), kind=kOutput, calls=%fused_computation.18 | convolution fusion | flops 134217728 | bytes 18874368 | tf_op jit(solution)/shard_map/wif,wjf->ijf/dot_general | solution.py:53
  139.8 12.9 %fusion.3 = bf16[128,128,256]{0,1,2:T(8,128)(2,1)} fusion(f32[256,128,128]{2,1,0:T(8,128)} %fusion.13, bf16[16,128,256]{1,2,0:T(8,128)(2,1)S(1)} %get-tuple-element.20, bf16[16,128,256]{1,2,0:T(8,128)(2,1)S(1)} %get-tuple-element.6), kind=kOutput, calls=%fused_computation.6 | convolution fusion | flops 142606336 | bytes 27262976 | tf_op jit(solution)/shard_map/wif,wjf->ijf/dot_general | solution.py:50
  152.7 13.5 %copy.39 = bf16[128,128,256]{2,1,0:T(8,128)(2,1)} copy(bf16[128,128,256]{0,1,2:T(8,128)(2,1)} %fusion.3) | data formatting | bytes 16777216 | tf_op jit(solution)/shard_map/add | solution.py:50
  166.1 12.9 %fusion.4 = bf16[128,128,256]{0,1,2:T(8,128)(2,1)} fusion(f32[256,128,128]{2,1,0:T(8,128)} %fusion.9, bf16[16,128,256]{1,2,0:T(8,128)(2,1)S(1)} %get-tuple-element.20, bf16[16,128,256]{1,2,0:T(8,128)(2,1)S(1)} %get-tuple-element.5), kind=kOutput, calls=%fused_computation.7 | convolution fusion | flops 142606336 | bytes 27262976 | tf_op jit(solution)/shard_map/wif,wjf->ijf/dot_general | solution.py:54
  179.1 13.5 %copy.44 = bf16[128,128,256]{2,1,0:T(8,128)(2,1)} copy(bf16[128,128,256]{0,1,2:T(8,128)(2,1)} %fusion.4) | data formatting | bytes 16777216 | tf_op jit(solution)/shard_map/sub | solution.py:54
  192.6 14.5 %convolution_convert_fusion = bf16[16384,256]{1,0:T(8,128)(2,1)} fusion(bf16[16384,256]{1,0:T(8,128)(2,1)} %bitcast.41, bf16[16384,256]{1,0:T(8,128)(2,1)} %bitcast.40, f32[512]{0:T(512)S(1)} %get-tuple-element.12, s32[256]{0:T(256)S(1)} %iota_add_fusion, s32[512]{0:T(512)S(1)} %pad_add_fusion, f32[512]{0:T(512)S(1)} %get-tuple-element.11, ...), kind=kOutput, calls=%fused_computation | convolution fusion | flops 4335075328 | bytes 25173504 | tf_op jit(solution)/shard_map/dot_general | solution.py:93
  (26 shorter events, 0.4 us)
Async XLA Ops:
  6.5 37.6 %copy-start = (bf16[16,8,2048]{2,1,0:T(8,128)(2,1)S(1)}, bf16[16,8,2048]{2,1,0:T(8,128)(2,1)}, u32[]{:S(2)}) copy-start(bf16[16,8,2048]{2,1,0:T(8,128)(2,1)} %param.4) | copy-start | bytes 1572868
  6.5 111.8 %all-gather.3.cloned.1.call-start = ((), (), s32[]{:S(2)}) async-start(), calls=%async_computation | async-start | bytes 2228224 | tf_op jit(solution)/shard_map/all_gather | solution.py:81
  44.2 34.6 %copy-start.2 = (s32[16,8]{0,1:T(8,128)S(1)}, s32[16,8]{0,1:T(8,128)}, u32[]{:S(2)}) copy-start(s32[16,8]{0,1:T(8,128)} %param.6) | copy-start | bytes 1540
  44.2 35.5 %copy-start.3 = (s32[16,2]{0,1:T(2,128)S(1)}, s32[16,2]{0,1:T(2,128)}, u32[]{:S(2)}) copy-start(s32[16,2]{0,1:T(2,128)} %param.7) | copy-start | bytes 388
  192.6 14.5 %copy-start.1 = (bf16[16,8,2048]{2,1,0:T(8,128)(2,1)S(1)}, bf16[16,8,2048]{2,1,0:T(8,128)(2,1)}, u32[]{:S(2)}) copy-start(bf16[16,8,2048]{2,1,0:T(8,128)(2,1)} %param.4) | copy-start | bytes 1572868
Sparse Core Ops, SparseCore 0:
  79.8 38.4 all-gather.2
